TPU v7x, 256 devices: a whole 4x4x8 slice. The times are simulated.
256 devices in a mesh: sec: 32 (over x, z), op: 8 (over y, core).
Axes of the slice: x: 4, y: 4, z: 8, core: 2. Of those that a mesh axis runs over, the one named last changes fastest.
Arguments:
- state_start: bfloat16 [64, 256, 256], P('sec'), may hold values from -60 to 60
- left_ops: bfloat16 [64, 64, 256, 256], P('op', 'sec'), may hold values from -0.375 to 0.375
- right_ops: bfloat16 [64, 64, 256, 256], P('op', 'sec'), may hold values from -0.046875 to 0.046875
- shift: float32 [64], P('sec'), may hold values from 0.2 to 2.2
- partner: int32 [64, 64], P('op', 'sec'), may hold values from 0 to 5
- kept: int32 [64], P('sec'), may hold values from 128 to 256
Outputs:
- state_final: bfloat16 [64, 256, 256], P('sec')
- new_ops: bfloat16 [64, 64, 256, 256], P('op', 'sec')
Inputs may be any that keep to these rules, and one draw needn't show every extreme that they name: `partner`: position in the window of 6 sector blocks.
All inputs are finite; a program needn't handle non-finite values.
Results may differ from a plain program's by a relative error of at most 0.015.
Values may be sent and summed in bfloat16 or wider, within the bound.
A program may use at most 64 MiB of HBM per device.

v0:
```python
import jax
import jax.numpy as jnp
from jax import lax
from jax.sharding import PartitionSpec as P

ITERS = 4
step_size = 0.5


def padded(cells, sides, width):
    for axis, dim in sides:
        count = lax.axis_size(axis)
        head = lax.slice_in_dim(cells, 0, width, axis=dim)
        tail = lax.slice_in_dim(cells, cells.shape[dim] - width, cells.shape[dim], axis=dim)
        cells = jnp.concatenate(
            [
                lax.ppermute(tail, axis, [(i, (i + 1) % count) for i in range(count)]),
                cells,
                lax.ppermute(head, axis, [((i + 1) % count, i) for i in range(count)]),
            ],
            axis=dim,
        )
    return cells


def shifted(block, axis, distance):
    devices = range(lax.axis_size(axis))
    route = [((i - distance) % len(devices), i) for i in devices]
    return lax.ppermute(block, axis, route)


def per_device(state_start, left_ops, right_ops, shift, partner, kept):
    sector_local = state_start.shape[0]
    width = state_start.shape[1]
    share_rows = width // lax.axis_size("op")
    share_start = lax.axis_index("op") * share_rows
    count = float(sector_local * lax.axis_size("sec") * width * width)
    shift_col = shift[:, None, None]
    state = state_start
    for iteration in range(ITERS):
        window = padded(state, (("sec", 0),), sector_local)
        sources = window[partner]
        halfway = jnp.einsum(
            "tbij,tbjk->tbik", left_ops, sources, preferred_element_type=jnp.float32
        ).astype(jnp.bfloat16)
        partial_sigma = jnp.einsum(
            "tbij,tbjk->bik", halfway, right_ops, preferred_element_type=jnp.float32
        )
        state_wide = state.astype(jnp.float32)
        state_part = lax.dynamic_slice_in_dim(state_wide, share_start, share_rows, 1)
        sigma = lax.psum(partial_sigma, "op") + shift_col * state_wide
        sigma_part = lax.dynamic_slice_in_dim(sigma, share_start, share_rows, 1)
        energy_sum, norm_sum, square_sum = lax.psum(
            (
                jnp.sum(state_part * sigma_part),
                jnp.sum(state_part * state_part),
                jnp.sum(sigma_part * sigma_part),
            ),
            ("sec", "op"),
        )
        ratio = energy_sum / norm_sum
        updated_part = state_part - step_size * (sigma_part - ratio * state_part)
        new_norm = lax.psum(jnp.sum(updated_part * updated_part), ("sec", "op"))
        factor = jnp.sqrt(count / new_norm)
        updated = state_wide - step_size * (sigma - ratio * state_wide)
        state = (updated * factor).astype(jnp.bfloat16)
    columns = jnp.arange(width, dtype=jnp.int32)
    keep_mask = (columns[None, :] < kept[:, None]).astype(jnp.bfloat16)
    kept_block = state * keep_mask[:, None, :]
    out_scale = 1.0 / float(width) ** 0.5
    projected = jnp.einsum(
        "tbij,bjk->tbik", left_ops, kept_block, preferred_element_type=jnp.float32
    ).astype(jnp.bfloat16)
    renormed = (
        jnp.einsum("bji,tbjk->tbik", kept_block, projected, preferred_element_type=jnp.float32)
        * out_scale
    ).astype(jnp.bfloat16)
    new_ops = shifted(renormed, "sec", 1)
    return (state, new_ops)


def solution(mesh):
    in_specs = (
        P("sec", None, None),
        P("op", "sec", None, None),
        P("op", "sec", None, None),
        P("sec"),
        P("op", "sec"),
        P("sec"),
    )
    out_specs = (P("sec", None, None), P("op", "sec", None, None))
    return jax.shard_map(
        per_device, mesh=mesh, in_specs=in_specs, out_specs=out_specs, check_vma=False
    )
```

profile of v0, /device:TPU:1, one launch (start us, length us, event | category | flops | bytes accessed | tf_op | source)
XLA Modules:
  0.0 1021.9 jit_solution(1389676207874550599)
XLA Ops:
  7.2 2.5 collective-permute-start
  9.8 6.2 collective-permute-start.1
  16.9 5.3 collective-permute-done
  23.2 2.0 gather_fusion
  25.2 4.3 fusion.47
  30.5 62.1 %all-reduce.9.cloned.1.call-done = f32[2,256,256]{2,1,0:T(8,128)} async-done(((f32[2,256,256]{2,1,0:T(8,128)}), f32[2,256,256]{2,1,0:T(8,128)}) %all-reduce.9.cloned.1.call-update) | async-done | bytes 524304 | tf_op jit(solution)/shard_map/psum | solution.py:51
  95.3 78.5 %all-reduce.3 = (f32[]{:T(128)}, f32[]{:T(128)}) all-reduce(f32[]{:T(128)} %get-tuple-element.13, f32[]{:T(128)} %get-tuple-element.12), channel_id=1, replica_groups=mesh['sec'=32,'op'=8] {'sec','op'}, use_global_device_ids=true, to_apply=%region_2.0 | all-reduce | flops 2 | bytes 16 | tf_op jit(solution)/shard_map/psum | solution.py:53
  176.5 73.4 %psum.115 = f32[]{:T(128)} all-reduce(f32[]{:T(128)} %multiply_reduce_fusion.9), channel_id=1, replica_groups=mesh['sec'=32,'op'=8] {'sec','op'}, use_global_device_ids=true, to_apply=%region_6.0 | all-reduce | flops 1 | bytes 8 | tf_op jit(solution)/shard_map/psum | solution.py:63
  251.6 2.2 collective-permute-start.3
  253.7 5.0 collective-permute-done.3
  258.8 5.2 collective-permute-done.2
  266.0 4.3 fusion.54
  270.4 57.5 %all-reduce.11.cloned.1.call-done = f32[2,256,256]{2,1,0:T(8,128)} async-done(((f32[2,256,256]{2,1,0:T(8,128)}), f32[2,256,256]{2,1,0:T(8,128)}) %all-reduce.11.cloned.1.call-update) | async-done | bytes 524304 | tf_op jit(solution)/shard_map/psum | solution.py:51
  330.6 78.5 %all-reduce.2 = (f32[]{:T(128)}, f32[]{:T(128)}) all-reduce(f32[]{:T(128)} %get-tuple-element.11, f32[]{:T(128)} %get-tuple-element.10), channel_id=1, replica_groups=mesh['sec'=32,'op'=8] {'sec','op'}, use_global_device_ids=true, to_apply=%region_9.0 | all-reduce | flops 2 | bytes 16 | tf_op jit(solution)/shard_map/psum | solution.py:53
  411.9 73.4 %psum.119 = f32[]{:T(128)} all-reduce(f32[]{:T(128)} %multiply_reduce_fusion.6), channel_id=1, replica_groups=mesh['sec'=32,'op'=8] {'sec','op'}, use_global_device_ids=true, to_apply=%region_13.0 | all-reduce | flops 1 | bytes 8 | tf_op jit(solution)/shard_map/psum | solution.py:63
  486.9 2.2 collective-permute-start.5
  489.1 5.0 collective-permute-done.5
  494.1 5.2 collective-permute-done.4
  501.4 4.3 fusion.61
  505.8 57.6 %all-reduce.13.cloned.1.call-done = f32[2,256,256]{2,1,0:T(8,128)} async-done(((f32[2,256,256]{2,1,0:T(8,128)}), f32[2,256,256]{2,1,0:T(8,128)}) %all-reduce.13.cloned.1.call-update) | async-done | bytes 524304 | tf_op jit(solution)/shard_map/psum | solution.py:51
  566.0 78.5 %all-reduce.1 = (f32[]{:T(128)}, f32[]{:T(128)}) all-reduce(f32[]{:T(128)} %get-tuple-element.9, f32[]{:T(128)} %get-tuple-element.8), channel_id=1, replica_groups=mesh['sec'=32,'op'=8] {'sec','op'}, use_global_device_ids=true, to_apply=%region_16.0 | all-reduce | flops 2 | bytes 16 | tf_op jit(solution)/shard_map/psum | solution.py:53
  647.3 73.4 %psum.123 = f32[]{:T(128)} all-reduce(f32[]{:T(128)} %multiply_reduce_fusion.3), channel_id=1, replica_groups=mesh['sec'=32,'op'=8] {'sec','op'}, use_global_device_ids=true, to_apply=%region_20.0 | all-reduce | flops 1 | bytes 8 | tf_op jit(solution)/shard_map/psum | solution.py:63
  722.3 2.2 collective-permute-start.7
  724.5 5.0 collective-permute-done.7
  729.5 5.2 collective-permute-done.6
  736.8 4.3 fusion.68
  741.1 57.6 %all-reduce.15.cloned.1.call-done = f32[2,256,256]{2,1,0:T(8,128)} async-done(((f32[2,256,256]{2,1,0:T(8,128)}), f32[2,256,256]{2,1,0:T(8,128)}) %all-reduce.15.cloned.1.call-update) | async-done | bytes 524304 | tf_op jit(solution)/shard_map/psum | solution.py:51
  801.4 78.5 %all-reduce = (f32[]{:T(128)}, f32[]{:T(128)}) all-reduce(f32[]{:T(128)} %get-tuple-element.7, f32[]{:T(128)} %get-tuple-element.6), channel_id=1, replica_groups=mesh['sec'=32,'op'=8] {'sec','op'}, use_global_device_ids=true, to_apply=%region_23.0 | all-reduce | flops 2 | bytes 16 | tf_op jit(solution)/shard_map/psum | solution.py:53
  882.7 73.4 %psum.127 = f32[]{:T(128)} all-reduce(f32[]{:T(128)} %multiply_reduce_fusion), channel_id=1, replica_groups=mesh['sec'=32,'op'=8] {'sec','op'}, use_global_device_ids=true, to_apply=%region_27.0 | all-reduce | flops 1 | bytes 8 | tf_op jit(solution)/shard_map/psum | solution.py:63
  957.0 4.3 fusion.40
  962.3 49.2 %collective-permute-done.8 = bf16[8,2,256,256]{2,3,0,1:T(8,128)(2,1)} collective-permute-done((bf16[8,2,256,256]{2,3,0,1:T(8,128)(2,1)}, bf16[8,2,256,256]{2,3,0,1:T(8,128)(2,1)}, u32[]{:S(2)}, u32[]{:S(2)}) %collective-permute-start.8) | collective-permute-done | bytes 2097184 | tf_op jit(solution)/shard_map/ppermute | solution.py:29
  1011.5 3.9 copy.19
  (52 shorter events, 29.6 us)
Async XLA Ops:
  7.2 18.0 %copy-start = (bf16[8,2,256,256]{3,2,1,0:T(8,128)(2,1)S(1)}, bf16[8,2,256,256]{3,2,1,0:T(8,128)(2,1)}, u32[]{:S(2)}) copy-start(bf16[8,2,256,256]{3,2,1,0:T(8,128)(2,1)} %param.8) | copy-start | bytes 6291460
  7.2 85.4 %all-reduce.9.cloned.1.call-start = ((), (), s32[]{:S(2)}) async-start(), calls=%async_computation | async-start | bytes 1048576 | tf_op jit(solution)/shard_map/psum | solution.py:51
  7.2 14.9 %collective-permute-start = (bf16[2,256,256]{2,1,0:T(8,128)(2,1)}, bf16[2,256,256]{2,1,0:T(8,128)(2,1)S(1)}, u32[]{:S(2)}, u32[]{:S(2)}) collective-permute-start(bf16[2,256,256]{2,1,0:T(8,128)(2,1)} %param.6), channel_id=1, source_target_pairs={{0,8},{8,16},{16,24},{24,32},{32,40},{40,48},{48,56},{56,64},{64,7... | collective-permute-start | bytes 786440 | tf_op jit(solution)/shard_map/ppermute | solution.py:17
  9.8 12.4 %collective-permute-start.1 = (bf16[2,256,256]{2,1,0:T(8,128)(2,1)}, bf16[2,256,256]{2,1,0:T(8,128)(2,1)S(1)}, u32[]{:S(2)}, u32[]{:S(2)}) collective-permute-start(bf16[2,256,256]{2,1,0:T(8,128)(2,1)} %param.6), channel_id=1, source_target_pairs={{8,0},{16,8},{24,16},{32,24},{40,32},{48,40},{56,48},{64,56},{72,6... | collective-permute-start | bytes 786440 | tf_op jit(solution)/shard_map/ppermute | solution.py:19
  25.2 4.4 copy-start.1
  25.2 67.4 %copy-start.3 = (f32[2]{0:T(128)S(1)}, f32[2]{0:T(128)}, u32[]{:S(2)}) copy-start(f32[2]{0:T(128)} %param.9) | copy-start | bytes 28
  29.6 298.4 %all-reduce.11.cloned.1.call-start = ((), (), s32[]{:S(2)}) async-start(), calls=%async_computation.1 | async-start | bytes 1048576 | tf_op jit(solution)/shard_map/psum | solution.py:51
  251.6 7.2 collective-permute-start.3
  253.7 10.2 collective-permute-start.2
  270.3 293.0 %all-reduce.13.cloned.1.call-start = ((), (), s32[]{:S(2)}) async-start(), calls=%async_computation.2 | async-start | bytes 1048576 | tf_op jit(solution)/shard_map/psum | solution.py:51
  486.9 7.2 collective-permute-start.5
  489.1 10.2 collective-permute-start.4
  505.7 293.0 %all-reduce.15.cloned.1.call-start = ((), (), s32[]{:S(2)}) async-start(), calls=%async_computation.3 | async-start | bytes 1048576 | tf_op jit(solution)/shard_map/psum | solution.py:51
  722.3 7.2 collective-permute-start.7
  724.5 10.2 collective-permute-start.6
  741.1 141.5 %copy-start.4 = (s32[2]{0:T(128)S(1)}, s32[2]{0:T(128)}, u32[]{:S(2)}) copy-start(s32[2]{0:T(128)} %param.11) | copy-start | bytes 28
  957.0 4.3 copy-start.2
  961.3 50.2 %collective-permute-start.8 = (bf16[8,2,256,256]{2,3,0,1:T(8,128)(2,1)}, bf16[8,2,256,256]{2,3,0,1:T(8,128)(2,1)}, u32[]{:S(2)}, u32[]{:S(2)}) collective-permute-start(bf16[8,2,256,256]{2,3,0,1:T(8,128)(2,1)} %fusion.40), channel_id=1, source_target_pairs={{248,0},{0,8},{8,16},{16,24},{24,32},{32,40},{40,48},{48,56},{56,6... | collective-permute-start | bytes 6291464 | tf_op jit(solution)/shard_map/ppermute | solution.py:29
Sparse Core Ops, SparseCore 0:
  29.7 62.8 all-reduce.8
  270.5 57.4 all-reduce.10
  505.8 57.4 all-reduce.12
  741.2 57.4 all-reduce.14
where the time goes:
time: 1020 us
  blocking collectives  608 us (60%)
  waiting for transfers between devices  320 us (31%)
  other arithmetic  22.3 us (2%)
  between operations  22.1 us (2%)
  matrix products  21.6 us (2%)
  starting transfers between devices  16.4 us (2%)
  local copies, waits for them, and re-layouts  12.1 us (1%)
    psum x4, blocking collectives, per_device(): lax.psum((jnp.sum(state_part * sigma_part), jnp.sum(state_part * state_pa...  314 us
    psum x4, blocking collectives, per_device(): new_norm = lax.psum(jnp.sum(updated_part * updated_part), ('sec', 'op'))  294 us
    psum x4, waiting for transfers between devices, per_device(): sigma = lax.psum(partial_sigma, 'op') + shift_col * state_wide  235 us
    ppermute x1, waiting for transfers between devices, shifted(): return lax.ppermute(block, axis, route)  49.2 us
    ppermute x4, waiting for transfers between devices, padded(): lax.ppermute(tail, axis, [(i, (i + 1) % count) for i in range(count)])  20.8 us
  transfers between devices with their start and end apart: 13, of which 12 were waited for; matrix products, arithmetic and copies ran while one was open for 0% of the time, Pallas kernels for 0%

commit v1 on v0

--- a/solution.py
+++ b/solution.py
@@ -51,12 +51,15 @@
         sigma = lax.psum(partial_sigma, "op") + shift_col * state_wide
         sigma_part = lax.dynamic_slice_in_dim(sigma, share_start, share_rows, 1)
         energy_sum, norm_sum, square_sum = lax.psum(
-            (
-                jnp.sum(state_part * sigma_part),
-                jnp.sum(state_part * state_part),
-                jnp.sum(sigma_part * sigma_part),
+            lax.psum(
+                (
+                    jnp.sum(state_part * sigma_part),
+                    jnp.sum(state_part * state_part),
+                    jnp.sum(sigma_part * sigma_part),
+                ),
+                "op",
             ),
-            ("sec", "op"),
+            "sec",
         )
         ratio = energy_sum / norm_sum
         updated_part = state_part - step_size * (sigma_part - ratio * state_part)

time: 1020 us -> 1070 us (1.049)
  blocking collectives: 608 us -> 651 us
    psum x4, blocking collectives: 314 us -> 60.6 us  [per_device(): lax.psum((jnp.sum(state_part * sigma_part), jnp.sum(state_part * state_pa...]
    psum x0 -> x4, blocking collectives: none -> 248 us  [per_device(): lax.psum(lax.psum((jnp.sum(state_part * sigma_part), jnp.sum(state_part *...]
    psum x4, blocking collectives: 294 us -> 343 us  [per_device(): new_norm = lax.psum(jnp.sum(updated_part * updated_part), ('sec', 'op'))]
where the time goes in v1:
time: 1070 us
  blocking collectives  651 us (61%)
  waiting for transfers between devices  317 us (30%)
  starting transfers between devices  22.7 us (2%)
  other arithmetic  22.2 us (2%)
  between operations  22.1 us (2%)
  matrix products  21.6 us (2%)
  local copies, waits for them, and re-layouts  12.1 us (1%)
    psum x4, blocking collectives, per_device(): new_norm = lax.psum(jnp.sum(updated_part * updated_part), ('sec', 'op'))  343 us
    psum x4, blocking collectives, per_device(): lax.psum(lax.psum((jnp.sum(state_part * sigma_part), jnp.sum(state_part *...  248 us
    psum x4, waiting for transfers between devices, per_device(): sigma = lax.psum(partial_sigma, 'op') + shift_col * state_wide  232 us
    psum x4, blocking collectives, per_device(): lax.psum((jnp.sum(state_part * sigma_part), jnp.sum(state_part * state_pa...  60.6 us
    ppermute x1, waiting for transfers between devices, shifted(): return lax.ppermute(block, axis, route)  48.4 us
  transfers between devices with their start and end apart: 13, of which 12 were waited for; matrix products, arithmetic and copies ran while one was open for 0% of the time, Pallas kernels for 0%

profile of v1, /device:TPU:1, one launch (start us, length us, event | category | flops | bytes accessed | tf_op | source)
XLA Modules:
  0.0 1068.5 jit_solution(11659142304094759222)
XLA Ops:
  9.8 6.2 collective-permute-start.1
  16.9 5.3 collective-permute-done
  25.2 4.3 fusion.47
  30.5 62.1 %all-reduce.13.cloned.1.call-done = f32[2,256,256]{2,1,0:T(8,128)} async-done(((f32[2,256,256]{2,1,0:T(8,128)}), f32[2,256,256]{2,1,0:T(8,128)}) %all-reduce.13.cloned.1.call-update) | async-done | bytes 524304 | tf_op jit(solution)/shard_map/psum | solution.py:51
  95.2 15.2 %all-reduce.7 = (f32[]{:T(128)}, f32[]{:T(128)}) all-reduce(f32[]{:T(128)} %get-tuple-element.13, f32[]{:T(128)} %get-tuple-element.12), channel_id=1, replica_groups=mesh['sec'=32,'op'=8] {'op'}, use_global_device_ids=true, to_apply=%region_2.0 | all-reduce | flops 2 | bytes 16 | tf_op jit(solution)/shard_map/psum | solution.py:54
  110.4 61.9 %all-reduce.3 = (f32[]{:T(128)}, f32[]{:T(128)}) all-reduce(f32[]{:T(128)} %get-tuple-element.28, f32[]{:T(128)} %get-tuple-element.29), channel_id=1, replica_groups=mesh['sec'=32,'op'=8] {'sec'}, use_global_device_ids=true, to_apply=%region_3.0 | all-reduce | flops 2 | bytes 16 | tf_op jit(solution)/shard_map/psum | solution.py:53
  175.0 85.8 %psum.173 = f32[]{:T(128)} all-reduce(f32[]{:T(128)} %multiply_reduce_fusion.9), channel_id=1, replica_groups=mesh['sec'=32,'op'=8] {'sec','op'}, use_global_device_ids=true, to_apply=%region_8.0 | all-reduce | flops 1 | bytes 8 | tf_op jit(solution)/shard_map/psum | solution.py:66
  262.4 4.0 collective-permute-start.3
  266.4 5.0 collective-permute-done.3
  271.4 5.2 collective-permute-done.2
  278.7 4.3 fusion.54
  283.1 56.7 %all-reduce.15.cloned.1.call-done = f32[2,256,256]{2,1,0:T(8,128)} async-done(((f32[2,256,256]{2,1,0:T(8,128)}), f32[2,256,256]{2,1,0:T(8,128)}) %all-reduce.15.cloned.1.call-update) | async-done | bytes 524304 | tf_op jit(solution)/shard_map/psum | solution.py:51
  342.4 15.1 %all-reduce.6 = (f32[]{:T(128)}, f32[]{:T(128)}) all-reduce(f32[]{:T(128)} %get-tuple-element.11, f32[]{:T(128)} %get-tuple-element.10), channel_id=1, replica_groups=mesh['sec'=32,'op'=8] {'op'}, use_global_device_ids=true, to_apply=%region_11.0 | all-reduce | flops 2 | bytes 16 | tf_op jit(solution)/shard_map/psum | solution.py:54
  357.5 61.9 %all-reduce.2 = (f32[]{:T(128)}, f32[]{:T(128)}) all-reduce(f32[]{:T(128)} %get-tuple-element.26, f32[]{:T(128)} %get-tuple-element.27), channel_id=1, replica_groups=mesh['sec'=32,'op'=8] {'sec'}, use_global_device_ids=true, to_apply=%region_12.0 | all-reduce | flops 2 | bytes 16 | tf_op jit(solution)/shard_map/psum | solution.py:53
  422.2 85.8 %psum.179 = f32[]{:T(128)} all-reduce(f32[]{:T(128)} %multiply_reduce_fusion.6), channel_id=1, replica_groups=mesh['sec'=32,'op'=8] {'sec','op'}, use_global_device_ids=true, to_apply=%region_17.0 | all-reduce | flops 1 | bytes 8 | tf_op jit(solution)/shard_map/psum | solution.py:66
  513.6 5.0 collective-permute-done.5
  518.6 5.2 collective-permute-done.4
  525.9 4.3 fusion.61
  530.3 56.7 %all-reduce.17.cloned.1.call-done = f32[2,256,256]{2,1,0:T(8,128)} async-done(((f32[2,256,256]{2,1,0:T(8,128)}), f32[2,256,256]{2,1,0:T(8,128)}) %all-reduce.17.cloned.1.call-update) | async-done | bytes 524304 | tf_op jit(solution)/shard_map/psum | solution.py:51
  589.6 15.3 %all-reduce.5 = (f32[]{:T(128)}, f32[]{:T(128)}) all-reduce(f32[]{:T(128)} %get-tuple-element.9, f32[]{:T(128)} %get-tuple-element.8), channel_id=1, replica_groups=mesh['sec'=32,'op'=8] {'op'}, use_global_device_ids=true, to_apply=%region_20.0 | all-reduce | flops 2 | bytes 16 | tf_op jit(solution)/shard_map/psum | solution.py:54
  604.9 61.9 %all-reduce.1 = (f32[]{:T(128)}, f32[]{:T(128)}) all-reduce(f32[]{:T(128)} %get-tuple-element.24, f32[]{:T(128)} %get-tuple-element.25), channel_id=1, replica_groups=mesh['sec'=32,'op'=8] {'sec'}, use_global_device_ids=true, to_apply=%region_21.0 | all-reduce | flops 2 | bytes 16 | tf_op jit(solution)/shard_map/psum | solution.py:53
  669.6 85.8 %psum.185 = f32[]{:T(128)} all-reduce(f32[]{:T(128)} %multiply_reduce_fusion.3), channel_id=1, replica_groups=mesh['sec'=32,'op'=8] {'sec','op'}, use_global_device_ids=true, to_apply=%region_26.0 | all-reduce | flops 1 | bytes 8 | tf_op jit(solution)/shard_map/psum | solution.py:66
  757.0 4.0 collective-permute-start.7
  761.0 5.0 collective-permute-done.7
  766.0 5.2 collective-permute-done.6
  773.3 4.3 fusion.68
  777.6 56.7 %all-reduce.19.cloned.1.call-done = f32[2,256,256]{2,1,0:T(8,128)} async-done(((f32[2,256,256]{2,1,0:T(8,128)}), f32[2,256,256]{2,1,0:T(8,128)}) %all-reduce.19.cloned.1.call-update) | async-done | bytes 524304 | tf_op jit(solution)/shard_map/psum | solution.py:51
  837.0 15.1 %all-reduce.4 = (f32[]{:T(128)}, f32[]{:T(128)}) all-reduce(f32[]{:T(128)} %get-tuple-element.7, f32[]{:T(128)} %get-tuple-element.6), channel_id=1, replica_groups=mesh['sec'=32,'op'=8] {'op'}, use_global_device_ids=true, to_apply=%region_29.0 | all-reduce | flops 2 | bytes 16 | tf_op jit(solution)/shard_map/psum | solution.py:54
  852.1 61.9 %all-reduce = (f32[]{:T(128)}, f32[]{:T(128)}) all-reduce(f32[]{:T(128)} %get-tuple-element.22, f32[]{:T(128)} %get-tuple-element.23), channel_id=1, replica_groups=mesh['sec'=32,'op'=8] {'sec'}, use_global_device_ids=true, to_apply=%region_30.0 | all-reduce | flops 2 | bytes 16 | tf_op jit(solution)/shard_map/psum | solution.py:53
  916.8 85.8 %psum.191 = f32[]{:T(128)} all-reduce(f32[]{:T(128)} %multiply_reduce_fusion), channel_id=1, replica_groups=mesh['sec'=32,'op'=8] {'sec','op'}, use_global_device_ids=true, to_apply=%region_35.0 | all-reduce | flops 1 | bytes 8 | tf_op jit(solution)/shard_map/psum | solution.py:66
  1003.5 4.3 fusion.40
  1009.6 48.4 %collective-permute-done.8 = bf16[8,2,256,256]{2,3,0,1:T(8,128)(2,1)} collective-permute-done((bf16[8,2,256,256]{2,3,0,1:T(8,128)(2,1)}, bf16[8,2,256,256]{2,3,0,1:T(8,128)(2,1)}, u32[]{:S(2)}, u32[]{:S(2)}) %collective-permute-start.8) | collective-permute-done | bytes 2097184 | tf_op jit(solution)/shard_map/ppermute | solution.py:29
  (56 shorter events, 42.8 us)
Async XLA Ops:
  7.2 18.0 %copy-start = (bf16[8,2,256,256]{3,2,1,0:T(8,128)(2,1)S(1)}, bf16[8,2,256,256]{3,2,1,0:T(8,128)(2,1)}, u32[]{:S(2)}) copy-start(bf16[8,2,256,256]{3,2,1,0:T(8,128)(2,1)} %param.8) | copy-start | bytes 6291460
  7.2 85.4 %all-reduce.13.cloned.1.call-start = ((), (), s32[]{:S(2)}) async-start(), calls=%async_computation | async-start | bytes 1048576 | tf_op jit(solution)/shard_map/psum | solution.py:51
  7.2 14.9 %collective-permute-start = (bf16[2,256,256]{2,1,0:T(8,128)(2,1)}, bf16[2,256,256]{2,1,0:T(8,128)(2,1)S(1)}, u32[]{:S(2)}, u32[]{:S(2)}) collective-permute-start(bf16[2,256,256]{2,1,0:T(8,128)(2,1)} %param.6), channel_id=1, source_target_pairs={{0,8},{8,16},{16,24},{24,32},{32,40},{40,48},{48,56},{56,64},{64,7... | collective-permute-start | bytes 786440 | tf_op jit(solution)/shard_map/ppermute | solution.py:17
  9.8 12.4 %collective-permute-start.1 = (bf16[2,256,256]{2,1,0:T(8,128)(2,1)}, bf16[2,256,256]{2,1,0:T(8,128)(2,1)S(1)}, u32[]{:S(2)}, u32[]{:S(2)}) collective-permute-start(bf16[2,256,256]{2,1,0:T(8,128)(2,1)} %param.6), channel_id=1, source_target_pairs={{8,0},{16,8},{24,16},{32,24},{40,32},{48,40},{56,48},{64,56},{72,6... | collective-permute-start | bytes 786440 | tf_op jit(solution)/shard_map/ppermute | solution.py:19
  25.2 4.4 copy-start.1
  25.2 67.4 %copy-start.3 = (f32[2]{0:T(128)S(1)}, f32[2]{0:T(128)}, u32[]{:S(2)}) copy-start(f32[2]{0:T(128)} %param.9) | copy-start | bytes 28
  29.6 310.2 %all-reduce.15.cloned.1.call-start = ((), (), s32[]{:S(2)}) async-start(), calls=%async_computation.1 | async-start | bytes 1048576 | tf_op jit(solution)/shard_map/psum | solution.py:51
  262.4 9.0 collective-permute-start.3
  266.4 10.2 collective-permute-start.2
  283.0 303.9 %all-reduce.17.cloned.1.call-start = ((), (), s32[]{:S(2)}) async-start(), calls=%async_computation.2 | async-start | bytes 1048576 | tf_op jit(solution)/shard_map/psum | solution.py:51
  509.6 9.0 collective-permute-start.5
  513.6 10.2 collective-permute-start.4
  530.2 304.1 %all-reduce.19.cloned.1.call-start = ((), (), s32[]{:S(2)}) async-start(), calls=%async_computation.3 | async-start | bytes 1048576 | tf_op jit(solution)/shard_map/psum | solution.py:51
  757.0 9.0 collective-permute-start.7
  761.0 10.2 collective-permute-start.6
  777.6 139.2 %copy-start.4 = (s32[2]{0:T(128)S(1)}, s32[2]{0:T(128)}, u32[]{:S(2)}) copy-start(s32[2]{0:T(128)} %param.11) | copy-start | bytes 28
  1003.5 4.3 copy-start.2
  1007.8 50.2 %collective-permute-start.8 = (bf16[8,2,256,256]{2,3,0,1:T(8,128)(2,1)}, bf16[8,2,256,256]{2,3,0,1:T(8,128)(2,1)}, u32[]{:S(2)}, u32[]{:S(2)}) collective-permute-start(bf16[8,2,256,256]{2,3,0,1:T(8,128)(2,1)} %fusion.40), channel_id=1, source_target_pairs={{248,0},{0,8},{8,16},{16,24},{24,32},{32,40},{40,48},{48,56},{56,6... | collective-permute-start | bytes 6291464 | tf_op jit(solution)/shard_map/ppermute | solution.py:29
Sparse Core Ops, SparseCore 0:
  29.7 62.8 all-reduce.12
  283.1 56.5 all-reduce.14
  530.3 56.5 all-reduce.16
  777.7 56.5 all-reduce.18
